TPU v7x, 32 devices: a whole 2x2x4 slice. The times are simulated.
32 devices in a mesh: slab: 8 (over z, y), mode: 4 (over x, core).
Axes of the slice: x: 2, y: 2, z: 4, core: 2. Of those that a mesh axis runs over, the one named last changes fastest.
Arguments:
- eigvec: bfloat16 [10240, 3, 1024], P('slab', None, 'mode'), may hold values from -6 to 6
- species: int32 [10240], P('slab'), may hold values from 0 to 3
- mode_cot: float32 [1024], P('mode'), may hold values from -4 to 4
- neighbours: int32 [10240, 16], P('slab'), may hold values from 0 to 2560, as said below
- pair_features: bfloat16 [163840, 128], P(('slab', 'mode')), may hold values from -130 to 130
- w_in: bfloat16 [128, 256], replicated, may hold values from -0.5 to 0.5
- b_in: float32 [256], replicated, may hold values from -3 to 3
- w_out: bfloat16 [9, 256], replicated, may hold values from -0.375 to 0.375
Outputs:
- features_grad: bfloat16 [163840, 128], P(('slab', 'mode'))
- grad_w_in: float32 [128, 256], replicated
- grad_b_in: float32 [256], replicated
- grad_w_out: float32 [9, 256], replicated
Inputs may be any that keep to these rules, and one draw needn't show every extreme that they name: `neighbours`: atom r of a slab (0 to 1279) lists extended indices from r to r + 1280; extended index x stands for atom (slab * 1280 + x - 640) mod 10240; the value 1280 + 2 * 640 marks an empty slot.
All inputs are finite; a program needn't handle non-finite values.
Results may differ from a plain program's by a relative error of at most 0.019.
Values may be sent and summed in bfloat16 or wider, within the bound.
A program may use at most 64 MiB of HBM per device.

v0:
```python
import jax
import jax.numpy as jnp
from jax import lax
from jax.sharding import PartitionSpec as P

MASS_TABLE = (1.35, 2.94, 2.79, 2.95)
CLIP_NORM = 100.0


def with_halo(block, sides, width):
    for axis, dim in sides:
        count = lax.axis_size(axis)
        forward = [(i, i + 1) for i in range(count - 1)]
        forward.append((count - 1, 0))
        backward = [(target, source) for source, target in forward]
        low = lax.ppermute(
            lax.slice_in_dim(block, block.shape[dim] - width, None, axis=dim), axis, forward
        )
        high = lax.ppermute(lax.slice_in_dim(block, 0, width, axis=dim), axis, backward)
        block = jnp.concatenate([low, block, high], axis=dim)
    return block


def atom_masses(species):
    kinds = jnp.arange(4, dtype=jnp.int32)
    onehot = (species[:, None] == kinds[None, :]).astype(jnp.float32)
    return jnp.sum(onehot * jnp.asarray(MASS_TABLE, jnp.float32)[None, :], axis=1)


def mlp_backward(features, pair_cot, w_in, b_in, w_out):
    preact = jnp.dot(features, w_in, preferred_element_type=jnp.float32) + b_in[None, :]
    sigmoid_pre = jax.nn.sigmoid(preact)
    hidden = (preact * sigmoid_pre).astype(jnp.bfloat16)
    hidden_cot = lax.dot_general(
        pair_cot, w_out, (((0,), (0,)), ((), ())), preferred_element_type=jnp.float32
    )
    pre_cot = (hidden_cot * sigmoid_pre * (1.0 + preact * (1.0 - sigmoid_pre))).astype(jnp.bfloat16)
    features_grad = lax.dot_general(
        pre_cot, w_in, (((1,), (1,)), ((), ())), preferred_element_type=jnp.float32
    ).astype(jnp.bfloat16)
    grad_w_in = lax.dot_general(
        features, pre_cot, (((0,), (0,)), ((), ())), preferred_element_type=jnp.float32
    )
    grad_b_in = jnp.sum(pre_cot.astype(jnp.float32), axis=0)
    grad_w_out = jnp.dot(pair_cot, hidden, preferred_element_type=jnp.float32)
    return (features_grad, grad_w_in, grad_b_in, grad_w_out)


def shards(eigvec, species, mode_cot, neighbours, pair_features, w_in, b_in, w_out):
    atom_count = eigvec.shape[0]
    local_modes = eigvec.shape[2]
    slot_count = neighbours.shape[1]
    rim_width = atom_count // 2
    block_size = min(128, atom_count)
    sentinel = atom_count + 2 * rim_width
    inv_root = lax.rsqrt(atom_masses(species))
    scaled = (eigvec.astype(jnp.float32) * inv_root[:, None, None]).astype(jnp.bfloat16)
    weighted = (scaled.astype(jnp.float32) * mode_cot[None, None, :]).astype(jnp.bfloat16)
    flat_rows = scaled.reshape(atom_count, 3 * local_modes)
    extended = with_halo(flat_rows, (("slab", 0),), rim_width)

    def fill_block(step, terms):
        offset = step * block_size
        left = lax.dynamic_slice_in_dim(weighted, offset, block_size, 0)
        own_rows = lax.dynamic_slice_in_dim(scaled, offset, block_size, 0)
        nbr_block = lax.dynamic_slice_in_dim(neighbours, offset, block_size, 0)
        live_mask = (nbr_block < sentinel).astype(jnp.float32)
        row_index = jnp.clip(nbr_block, 0, sentinel - 1)
        partners = jnp.take(extended, row_index.reshape(-1), axis=0).reshape(
            block_size, slot_count * 3, local_modes
        )
        pair_raw = lax.dot_general(
            left, partners, (((2,), (2,)), ((0,), (0,))), preferred_element_type=jnp.float32
        )
        pair_terms = jnp.transpose(
            pair_raw.reshape(block_size, 3, slot_count, 3), (1, 3, 0, 2)
        ).reshape(9, block_size, slot_count)
        self_raw = lax.dot_general(
            left, own_rows, (((2,), (2,)), ((0,), (0,))), preferred_element_type=jnp.float32
        )
        self_terms = jnp.transpose(self_raw, (1, 2, 0)).reshape(9, block_size)
        block_terms = (pair_terms - self_terms[:, :, None]) * live_mask[None]
        return lax.dynamic_update_slice_in_dim(terms, block_terms, offset, 1)

    terms = lax.fori_loop(
        0, atom_count // block_size, fill_block, jnp.zeros((9, atom_count, slot_count), jnp.float32)
    )
    flat = terms.reshape(9, atom_count * slot_count)
    summed = lax.psum_scatter(flat.astype(jnp.bfloat16), "mode", scatter_dimension=1, tiled=True)
    features_grad, part_w_in, part_b_in, part_w_out = mlp_backward(
        pair_features, summed, w_in, b_in, w_out
    )
    raw_w_in, raw_b_in, raw_w_out = lax.psum((part_w_in, part_b_in, part_w_out), ("slab", "mode"))
    norm_sq = (
        jnp.sum(raw_w_in * raw_w_in) + jnp.sum(raw_b_in * raw_b_in) + jnp.sum(raw_w_out * raw_w_out)
    )
    factor = jnp.minimum(1.0, CLIP_NORM / jnp.sqrt(norm_sq + 1e-06))
    return (features_grad, raw_w_in * factor, raw_b_in * factor, raw_w_out * factor)


def solution(mesh):
    return jax.shard_map(
        shards,
        mesh=mesh,
        in_specs=(
            P("slab", None, "mode"),
            P("slab"),
            P("mode"),
            P("slab", None),
            P(("slab", "mode"), None),
            P(),
            P(),
            P(),
        ),
        out_specs=(P(("slab", "mode"), None), P(), P(), P()),
        check_vma=False,
    )
```

profile of v0, /device:TPU:0, one launch (start us, length us, event | category | flops | bytes accessed | tf_op | source)
XLA Modules:
  0.0 602.7 jit_solution(6333406218551157884)
XLA Ops:
  7.3 4.1 copy.62
  11.4 3.5 multiply_convert_fusion.1
  16.4 3.0 collective-permute-start
  19.4 3.0 collective-permute-start.1
  22.4 39.4 %collective-permute-done = bf16[640,768]{0,1:T(8,128)(2,1)} collective-permute-done((bf16[640,768]{0,1:T(8,128)(2,1)}, bf16[640,768]{0,1:T(8,128)(2,1)}, u32[]{:S(2)}, u32[]{:S(2)}) %collective-permute-start) | collective-permute-done | bytes 983072 | tf_op jit(solution)/shard_map/ppermute | solution.py:16
  61.7 2.2 collective-permute-done.1
  64.0 3.2 pad_maximum_fusion
  67.2 6.3 %copy.64 = bf16[2560,768]{1,0:T(8,128)(2,1)} copy(bf16[2560,768]{0,1:T(8,128)(2,1)} %pad_maximum_fusion) | data formatting | bytes 7864320 | tf_op jit(solution)/shard_map/while | solution.py:85
  74.2 341.7 %while.13 = (s32[]{:T(128)}, bf16[9,1280,16]{1,2,0:T(8,128)(2,1)}, bf16[1280,3,256]{0,2,1:T(8,128)(2,1)}, s32[1280,16]{0,1:T(8,128)}, bf16[2560,768]{1,0:T(8,128...) while((s32[]{:T(128)}, bf16[9,1280,16]{1,2,0:T(8,128)(2,1)}, ...), condition=%wide.region_2.3_spmd, body=%wide.region_1.2_spmd.sunk | while | flops 11681798 | bytes 18693280 | solution.py:85
  75.1 12.8 %gather_fusion = bf16[2048,768]{1,0:T(8,128)(2,1)} fusion(bf16[2560,768]{1,0:T(8,128)(2,1)} %get-tuple-element.260, s32[2048]{0:T(1024)S(1)} %broadcast_clamp_fusion.2), kind=kCustom, calls=%fused_computation.clone.1 | custom fusion | bytes 6299648 | tf_op jit(solution)/shard_map/while/body/eval_jaxpr/jit(_take)/gather | solution.py:69
  88.0 5.9 gather.15
  97.5 3.7 fusion.32
  109.3 12.8 %gather_fusion = bf16[2048,768]{1,0:T(8,128)(2,1)} fusion(bf16[2560,768]{1,0:T(8,128)(2,1)} %get-tuple-element.260, s32[2048]{0:T(1024)S(1)} %broadcast_clamp_fusion.2), kind=kCustom, calls=%fused_computation.clone.1 | custom fusion | bytes 6299648 | tf_op jit(solution)/shard_map/while/body/eval_jaxpr/jit(_take)/gather | solution.py:69
  122.1 5.9 gather.15
  131.6 3.7 fusion.32
  143.5 12.8 %gather_fusion = bf16[2048,768]{1,0:T(8,128)(2,1)} fusion(bf16[2560,768]{1,0:T(8,128)(2,1)} %get-tuple-element.260, s32[2048]{0:T(1024)S(1)} %broadcast_clamp_fusion.2), kind=kCustom, calls=%fused_computation.clone.1 | custom fusion | bytes 6299648 | tf_op jit(solution)/shard_map/while/body/eval_jaxpr/jit(_take)/gather | solution.py:69
  156.3 5.9 gather.15
  165.8 3.7 fusion.32
  177.6 12.8 %gather_fusion = bf16[2048,768]{1,0:T(8,128)(2,1)} fusion(bf16[2560,768]{1,0:T(8,128)(2,1)} %get-tuple-element.260, s32[2048]{0:T(1024)S(1)} %broadcast_clamp_fusion.2), kind=kCustom, calls=%fused_computation.clone.1 | custom fusion | bytes 6299648 | tf_op jit(solution)/shard_map/while/body/eval_jaxpr/jit(_take)/gather | solution.py:69
  190.5 5.9 gather.15
  200.0 3.7 fusion.32
  211.8 12.8 %gather_fusion = bf16[2048,768]{1,0:T(8,128)(2,1)} fusion(bf16[2560,768]{1,0:T(8,128)(2,1)} %get-tuple-element.260, s32[2048]{0:T(1024)S(1)} %broadcast_clamp_fusion.2), kind=kCustom, calls=%fused_computation.clone.1 | custom fusion | bytes 6299648 | tf_op jit(solution)/shard_map/while/body/eval_jaxpr/jit(_take)/gather | solution.py:69
  224.6 5.9 gather.15
  234.1 3.7 fusion.32
  246.0 12.8 %gather_fusion = bf16[2048,768]{1,0:T(8,128)(2,1)} fusion(bf16[2560,768]{1,0:T(8,128)(2,1)} %get-tuple-element.260, s32[2048]{0:T(1024)S(1)} %broadcast_clamp_fusion.2), kind=kCustom, calls=%fused_computation.clone.1 | custom fusion | bytes 6299648 | tf_op jit(solution)/shard_map/while/body/eval_jaxpr/jit(_take)/gather | solution.py:69
  258.8 5.9 gather.15
  268.3 3.7 fusion.32
  280.1 12.8 %gather_fusion = bf16[2048,768]{1,0:T(8,128)(2,1)} fusion(bf16[2560,768]{1,0:T(8,128)(2,1)} %get-tuple-element.260, s32[2048]{0:T(1024)S(1)} %broadcast_clamp_fusion.2), kind=kCustom, calls=%fused_computation.clone.1 | custom fusion | bytes 6299648 | tf_op jit(solution)/shard_map/while/body/eval_jaxpr/jit(_take)/gather | solution.py:69
  293.0 5.9 gather.15
  302.5 3.7 fusion.32
  314.3 12.8 %gather_fusion = bf16[2048,768]{1,0:T(8,128)(2,1)} fusion(bf16[2560,768]{1,0:T(8,128)(2,1)} %get-tuple-element.260, s32[2048]{0:T(1024)S(1)} %broadcast_clamp_fusion.2), kind=kCustom, calls=%fused_computation.clone.1 | custom fusion | bytes 6299648 | tf_op jit(solution)/shard_map/while/body/eval_jaxpr/jit(_take)/gather | solution.py:69
  327.1 5.9 gather.15
  336.6 3.7 fusion.32
  348.5 12.8 %gather_fusion = bf16[2048,768]{1,0:T(8,128)(2,1)} fusion(bf16[2560,768]{1,0:T(8,128)(2,1)} %get-tuple-element.260, s32[2048]{0:T(1024)S(1)} %broadcast_clamp_fusion.2), kind=kCustom, calls=%fused_computation.clone.1 | custom fusion | bytes 6299648 | tf_op jit(solution)/shard_map/while/body/eval_jaxpr/jit(_take)/gather | solution.py:69
  361.3 5.9 gather.15
  370.8 3.7 fusion.32
  382.6 12.8 %gather_fusion = bf16[2048,768]{1,0:T(8,128)(2,1)} fusion(bf16[2560,768]{1,0:T(8,128)(2,1)} %get-tuple-element.260, s32[2048]{0:T(1024)S(1)} %broadcast_clamp_fusion.2), kind=kCustom, calls=%fused_computation.clone.1 | custom fusion | bytes 6299648 | tf_op jit(solution)/shard_map/while/body/eval_jaxpr/jit(_take)/gather | solution.py:69
  395.5 5.9 gather.15
  405.0 3.7 fusion.32
  415.9 3.6 copy.66
  419.5 11.8 %convert_element_type.43 = bf16[9,20480]{1,0:T(8,128)(2,1)} reshape(bf16[9,1280,16]{2,1,0:T(8,128)(2,1)} %copy.66) | data formatting | bytes 737280 | tf_op jit(solution)/shard_map/convert_element_type | solution.py:89
  431.6 3.1 convolution_add_fusion
  434.7 19.2 %reduce-scatter.2.cloned.1.call-done = bf16[9,5120]{1,0:T(8,128)(2,1)} async-done(((bf16[9,20480]{1,0:T(8,128)(2,1)}), bf16[9,5120]{1,0:T(8,128)(2,1)}) %reduce-scatter.2.cloned.1.call-update) | async-done | bytes 92176 | tf_op jit(solution)/shard_map/reduce_scatter | solution.py:89
  453.9 4.2 convert_reduce_fusion
  461.2 3.7 convolution_convert_fusion
  464.9 4.0 fusion.8
  468.9 39.5 %all-reduce = (f32[256]{0:T(256)S(1)}, f32[9,256]{1,0:T(8,128)S(1)}) all-reduce(f32[256]{0:T(256)S(1)} %get-tuple-element.187, f32[9,256]{1,0:T(8,128)S(1)} %fusion.8), channel_id=1, replica_groups=mesh['slab'=8,'mode'=4] {'slab','mode'}, use_global_device_ids=true, to_apply=%region_7.8 | all-reduce | flops 2560 | bytes 20480 | tf_op jit(solution)/shard_map/psum | solution.py:93
  509.5 80.0 %all-reduce.3.cloned.1.call-done = f32[128,256]{0,1:T(8,128)} async-done(((f32[128,256]{0,1:T(8,128)}), f32[128,256]{0,1:T(8,128)}) %all-reduce.3.cloned.1.call-update) | async-done | bytes 131088 | tf_op jit(solution)/shard_map/psum | solution.py:93
  (214 shorter events, 128.7 us)
Async XLA Ops:
  7.2 424.4 %copy-start = (bf16[5120,128]{1,0:T(8,128)(2,1)S(1)}, bf16[5120,128]{1,0:T(8,128)(2,1)}, u32[]{:S(2)}) copy-start(bf16[5120,128]{1,0:T(8,128)(2,1)} %param.15) | copy-start | bytes 3932164
  7.2 4.1 copy-start.6
  7.2 4.1 copy-start.3
  7.2 4.2 copy-start.5
  7.2 446.7 %reduce-scatter.2.cloned.1.call-start = ((), (), s32[]{:S(2)}) async-start(), calls=%async_computation.1 | async-start | bytes 819200 | tf_op jit(solution)/shard_map/reduce_scatter | solution.py:89
  16.4 45.4 %collective-permute-start = (bf16[640,768]{0,1:T(8,128)(2,1)}, bf16[640,768]{0,1:T(8,128)(2,1)}, u32[]{:S(2)}, u32[]{:S(2)}) collective-permute-start(bf16[640,768]{0,1:T(8,128)(2,1)} %bitcast.4), channel_id=1, source_target_pairs={{0,4},{4,8},{8,12},{12,16},{16,20},{20,24},{24,28},{28,0},{1,5},{5... | collective-permute-start | bytes 2949128 | tf_op jit(solution)/shard_map/ppermute | solution.py:16
  19.4 44.6 %collective-permute-start.1 = (bf16[640,768]{0,1:T(8,128)(2,1)}, bf16[640,768]{0,1:T(8,128)(2,1)}, u32[]{:S(2)}, u32[]{:S(2)}) collective-permute-start(bf16[640,768]{0,1:T(8,128)(2,1)} %bitcast.6), channel_id=1, source_target_pairs={{4,0},{8,4},{12,8},{16,12},{20,16},{24,20},{28,24},{0,28},{5,1},{9... | collective-permute-start | bytes 2949128 | tf_op jit(solution)/shard_map/ppermute | solution.py:19
  415.9 15.7 %copy-start.2 = (bf16[128,256]{1,0:T(8,128)(2,1)S(1)}, bf16[128,256]{1,0:T(8,128)(2,1)}, u32[]{:S(2)}) copy-start(bf16[128,256]{1,0:T(8,128)(2,1)} %param.16) | copy-start | bytes 196612
  415.9 15.7 %copy-start.4 = (f32[256]{0:T(256)S(1)}, f32[256]{0:T(256)}, u32[]{:S(2)}) copy-start(f32[256]{0:T(256)} %param.17) | copy-start | bytes 3076
  431.3 22.6 %copy-start.8 = (bf16[9,256]{1,0:T(8,128)(2,1)S(1)}, bf16[9,256]{1,0:T(8,128)(2,1)}, u32[]{:S(2)}) copy-start(bf16[9,256]{1,0:T(8,128)(2,1)} %param.18) | copy-start | bytes 13828
  431.3 158.2 %all-reduce.3.cloned.1.call-start = ((), (), s32[]{:S(2)}) async-start(), calls=%async_computation.2 | async-start | bytes 262144 | tf_op jit(solution)/shard_map/psum | solution.py:93
  458.1 1.5 copy-start.1
  461.2 3.7 copy-start.7
Sparse Core Ops, SparseCore 0:
  431.4 22.4 reduce-scatter.1
  465.0 124.4 all-reduce.2
where the time goes:
time: 607 us; the launch traced here: 603 us
  local copies, waits for them, and re-layouts  301 us (50%)
  waiting for transfers between devices  141 us (23%)
  matrix products  73.4 us (12%)
  blocking collectives  39.5 us (7%)
  other arithmetic  25.4 us (4%)
  between operations  16.1 us (3%)
  starting transfers between devices  6.3 us (1%)
    gather x20, local copies, waits for them, and re-layouts, fill_block(): jnp.take(extended, row_index.reshape(-1), axis=0)  187 us
    psum x1, waiting for transfers between devices, shards(): lax.psum((part_w_in, part_b_in, part_w_out), ('slab', 'mode'))  80 us
    psum x1, blocking collectives, shards(): lax.psum((part_w_in, part_b_in, part_w_out), ('slab', 'mode'))  39.5 us
    ppermute x1, waiting for transfers between devices, with_halo(): lax.ppermute(lax.slice_in_dim(block, block.shape[dim] - width, None, axis...  39.4 us
    dot_general x10, matrix products, fill_block(): lax.dot_general(left, partners, (((2,), (2,)), ((0,), (0,))), preferred_e...  36.9 us
    dynamic_slice x20, local copies, waits for them, and re-layouts, fill_block(): own_rows = lax.dynamic_slice_in_dim(scaled, offset, block_size, 0)  25.4 us
    dot_general x10, matrix products, fill_block(): lax.dot_general(left, own_rows, (((2,), (2,)), ((0,), (0,))), preferred_e...  20 us
    reduce_scatter x1, waiting for transfers between devices, shards(): lax.psum_scatter(flat.astype(jnp.bfloat16), 'mode', scatter_dimension=1,...  19.2 us
  transfers between devices with their start and end apart: 4, of which 4 were waited for; matrix products, arithmetic and copies ran while one was open for 1% of the time, Pallas kernels for 0%

commit v1 on v0

v1 whole, which is shorter than its diff:
```python
import functools

import jax
import jax.numpy as jnp
import numpy as np
from jax import lax
from jax.experimental import pallas as pl
from jax.experimental.pallas import tpu as pltpu
from jax.sharding import PartitionSpec as P

MASS_TABLE = (1.35, 2.94, 2.79, 2.95)
CLIP_NORM = 100.0
TILE = 128
VMEM_LIMIT = 60 * 1024 * 1024
MESH = pl.DeviceIdType.MESH
VMEM = pl.BlockSpec(memory_space=pltpu.VMEM)
SMEM = pl.BlockSpec(memory_space=pltpu.SMEM)


def inverse_root_mass(species):
    kinds = jnp.arange(4, dtype=jnp.int32)
    onehot = (species[:, None] == kinds[None, :]).astype(jnp.float32)
    masses = jnp.sum(onehot * jnp.asarray(MASS_TABLE, jnp.float32)[None, :], axis=1)
    return lax.rsqrt(masses)


def task_table(tasks):
    tasks = list(tasks)
    while len(tasks) % 2:
        tasks.append((tasks[-1][0], tasks[-1][1], -1))
    tasks.append((tasks[-1][0], tasks[-1][1], -1))
    return np.asarray(tasks, np.int32).T.copy()


def rows_of(block):
    return pl.ds(pl.multiple_of(block * TILE, TILE), TILE)


def band_tasks(table, own_ref, partner_ref, cot_ref, low_ref, high_ref, total_ref, even_ref, odd_ref):
    count = table.shape[1] - 1

    def product(task, dest):
        block, partner = table[0, task], table[1, task]
        cot = cot_ref[...]
        left = jnp.concatenate(
            [(own_ref[a, rows_of(block), :].astype(jnp.float32) * cot).astype(jnp.bfloat16) for a in range(3)], axis=0
        )
        right = jnp.concatenate([partner_ref[b, rows_of(partner), :] for b in range(3)], axis=0)
        dest[...] = lax.dot_general(left, right, (((1,), (1,)), ((), ())), preferred_element_type=jnp.float32)

    def select(task, source):
        block, distance = table[0, task], table[2, task]
        first = pl.multiple_of(block * TILE, TILE)
        for group in range(TILE // 8):
            rows = pl.ds(first + 8 * group, 8)
            lane = low_ref[rows, :]
            hit = high_ref[rows, :] == distance
            for a in range(3):
                for b in range(3):
                    values = source[a * TILE + 8 * group : a * TILE + 8 * group + 8, b * TILE : (b + 1) * TILE]
                    picked = jnp.take_along_axis(values, lane, axis=1, mode="promise_in_bounds")
                    total_ref[3 * a + b, rows, :] = jnp.where(hit, picked, total_ref[3 * a + b, rows, :])

    product(0, even_ref)

    def step(pair, _):
        product(2 * pair + 1, odd_ref)
        select(2 * pair, even_ref)
        product(2 * pair + 2, even_ref)
        select(2 * pair + 1, odd_ref)
        return 0

    lax.fori_loop(0, count // 2, step, 0)


def slot_tables(nbr_ref, low_ref, high_ref, block):
    slots = nbr_ref[:, rows_of(block)]
    spread = jnp.transpose(jnp.concatenate([slots] * (TILE // slots.shape[0]), axis=0))
    offset = spread - block * TILE
    low_ref[rows_of(block), :] = offset & (TILE - 1)
    high_ref[rows_of(block), :] = lax.shift_right_arithmetic(offset, 7)
    return spread


def packed(total_ref, block, slot_count):
    lanes = lax.broadcasted_iota(jnp.int32, (TILE, TILE), 1)
    position = lanes // slot_count
    first = jnp.zeros((TILE, TILE), jnp.float32)
    for part in range(8):
        first = jnp.where(position == part, total_ref[part, rows_of(block), :], first)
    last = jnp.where(position == 0, total_ref[8, rows_of(block), :], 0.0)
    return first, last


def own_kernel(table, own_ref, cot_ref, nbr_ref, out_ref, low_ref, high_ref, total_ref, even_ref, odd_ref):
    atom_count = own_ref.shape[1]
    slot_count = nbr_ref.shape[0]
    blocks = atom_count // TILE
    sentinel = 2 * atom_count

    def begin(block, _):
        slot_tables(nbr_ref, low_ref, high_ref, block)
        cot = cot_ref[...]
        own = [own_ref[b, rows_of(block), :].astype(jnp.float32) for b in range(3)]
        for a in range(3):
            left = (own[a] * cot).astype(jnp.bfloat16).astype(jnp.float32)
            for b in range(3):
                same = jnp.sum(left * own[b], axis=1, keepdims=True)
                total_ref[3 * a + b, rows_of(block), :] = jnp.zeros((TILE, TILE), jnp.float32)
                total_ref[9 + 3 * a + b, rows_of(block), :] = jnp.broadcast_to(same, (TILE, TILE))
        return 0

    lax.fori_loop(0, blocks, begin, 0)
    band_tasks(table, own_ref, own_ref, cot_ref, low_ref, high_ref, total_ref, even_ref, odd_ref)

    def finish(block, _):
        live = (high_ref[rows_of(block), :] * TILE + low_ref[rows_of(block), :] + block * TILE) < sentinel
        first, last = packed(total_ref, block, slot_count)
        self_first, self_last = packed(total_ref.at[9:18], block, slot_count)
        out_ref[rows_of(block), 0:TILE] = jnp.where(live, first - self_first, 0.0)
        out_ref[rows_of(block), TILE : 2 * TILE] = jnp.where(live, last - self_last, 0.0)
        return 0

    lax.fori_loop(0, blocks, finish, 0)


def rim_kernel(low_table, high_table, own_ref, low_rim, high_rim, cot_ref, nbr_ref, part_ref, out_ref,
               low_ref, high_ref, total_ref, even_ref, odd_ref):
    atom_count = own_ref.shape[1]
    slot_count = nbr_ref.shape[0]
    blocks = atom_count // TILE

    def begin(block, _):
        slot_tables(nbr_ref, low_ref, high_ref, block)
        for part in range(9):
            total_ref[part, rows_of(block), :] = jnp.zeros((TILE, TILE), jnp.float32)
        return 0

    lax.fori_loop(0, blocks, begin, 0)
    band_tasks(low_table, own_ref, low_rim, cot_ref, low_ref, high_ref, total_ref, even_ref, odd_ref)
    band_tasks(high_table, own_ref, high_rim, cot_ref, low_ref, high_ref, total_ref, even_ref, odd_ref)

    def finish(block, _):
        first, last = packed(total_ref, block, slot_count)
        rows = rows_of(block)
        out_ref[rows, 0:TILE] = (part_ref[rows, 0:TILE] + first).astype(jnp.bfloat16)
        out_ref[rows, TILE : 2 * TILE] = (part_ref[rows, TILE : 2 * TILE] + last).astype(jnp.bfloat16)
        return 0

    lax.fori_loop(0, blocks, finish, 0)


def scatter_kernel(groups, in_ref, out_ref, held, send_sem, recv_sem):
    slab = lax.axis_index("slab")
    me = lax.axis_index("mode")
    barrier = pltpu.get_barrier_semaphore()
    for hop in range(1, groups):
        pl.semaphore_signal(barrier, inc=1, device_id=(slab, lax.rem(me + hop, groups)), device_id_type=MESH)
    pl.semaphore_wait(barrier, groups - 1)
    copies = []
    for hop in range(1, groups):
        peer = lax.rem(me + hop, groups)
        copies.append(pltpu.make_async_remote_copy(
            src_ref=in_ref.at[peer], dst_ref=held.at[hop - 1], send_sem=send_sem.at[hop - 1],
            recv_sem=recv_sem.at[hop - 1], device_id=(slab, peer), device_id_type=MESH))
    for copy in copies:
        copy.start()
    total = in_ref[me].astype(jnp.float32)
    for copy in copies:
        copy.wait()
    for hop in range(1, groups):
        total = total + held[hop - 1].astype(jnp.float32)
    out_ref[...] = total


def mlp_kernel(slot_count, x_ref, cot_ref, w_in_ref, b_in_ref, w_rep_ref, grad_ref, sums_ref, w_out_sum):
    rows = min(512, x_ref.shape[0])
    atoms = rows // slot_count
    features = x_ref.shape[1]
    hidden_width = w_in_ref.shape[1]
    width = cot_ref.shape[1]
    sums_ref[...] = jnp.zeros_like(sums_ref)
    w_out_sum[...] = jnp.zeros_like(w_out_sum)
    row = lax.broadcasted_iota(jnp.int32, (rows, width), 0)
    lane = lax.broadcasted_iota(jnp.int32, (rows, width), 1)
    keep = lax.rem(row, slot_count) == lax.rem(lane, slot_count)

    def step(index, _):
        here = pl.ds(pl.multiple_of(index * rows, rows), rows)
        x = x_ref[here, :]
        preact = jnp.dot(x, w_in_ref[...], preferred_element_type=jnp.float32) + b_in_ref[...]
        gate = jax.nn.sigmoid(preact)
        hidden = (preact * gate).astype(jnp.bfloat16)
        block = cot_ref[pl.ds(pl.multiple_of(index * atoms, atoms), atoms), :]
        spread = jnp.broadcast_to(block[:, None, :], (atoms, slot_count, width)).reshape(rows, width)
        spread = jnp.where(keep, spread, 0.0).astype(jnp.bfloat16)
        hidden_cot = jnp.dot(spread, w_rep_ref[...], preferred_element_type=jnp.float32)
        pre_cot = (hidden_cot * gate * (1.0 + preact * (1.0 - gate))).astype(jnp.bfloat16)
        grad_ref[here, :] = lax.dot_general(
            pre_cot, w_in_ref[...], (((1,), (1,)), ((), ())), preferred_element_type=jnp.float32
        ).astype(jnp.bfloat16)
        sums_ref[0:features, :] += lax.dot_general(
            x, pre_cot, (((0,), (0,)), ((), ())), preferred_element_type=jnp.float32)
        sums_ref[features : features + 1, :] += jnp.sum(pre_cot.astype(jnp.float32), axis=0, keepdims=True)
        w_out_sum[...] += lax.dot_general(
            spread, hidden, (((0,), (0,)), ((), ())), preferred_element_type=jnp.float32)
        return 0

    lax.fori_loop(0, x_ref.shape[0] // rows, step, 0)
    for part in range(9):
        sums_ref[features + 1 + part : features + 2 + part, :] = jnp.sum(
            w_out_sum[part * slot_count : (part + 1) * slot_count, :], axis=0, keepdims=True)


def total_kernel(slabs, groups, features, in_ref, w_in_out, b_in_out, w_out_out,
                 held, mine, everyone, send_sem, recv_sem, back_send, back_recv):
    count = slabs * groups
    owners = in_ref.shape[0]
    me = lax.axis_index("slab") * groups + lax.axis_index("mode")

    def device(index):
        return (index // groups, lax.rem(index, groups))

    barrier = pltpu.get_barrier_semaphore()

    def greet(hop, _):
        pl.semaphore_signal(barrier, inc=1, device_id=device(lax.rem(me + hop, count)), device_id_type=MESH)
        return 0

    lax.fori_loop(1, count, greet, 0)
    pl.semaphore_wait(barrier, count - 1)

    def to_owner(owner):
        return pltpu.make_async_remote_copy(
            src_ref=in_ref.at[owner], dst_ref=held.at[me], send_sem=send_sem.at[owner],
            recv_sem=recv_sem.at[me], device_id=device(owner), device_id_type=MESH)

    def from_source(source):
        return pltpu.make_async_remote_copy(
            src_ref=in_ref.at[0], dst_ref=held.at[source], send_sem=send_sem.at[0],
            recv_sem=recv_sem.at[source], device_id=device(source), device_id_type=MESH)

    def to_all(target):
        return pltpu.make_async_remote_copy(
            src_ref=mine, dst_ref=everyone.at[me], send_sem=back_send.at[target],
            recv_sem=back_recv.at[me], device_id=device(target), device_id_type=MESH)

    def from_owner(owner):
        return pltpu.make_async_remote_copy(
            src_ref=mine, dst_ref=everyone.at[owner], send_sem=back_send.at[0],
            recv_sem=back_recv.at[owner], device_id=device(owner), device_id_type=MESH)

    def others(length, act):
        def body(index, _):
            @pl.when(index != me)
            def _():
                act(index)
            return 0
        lax.fori_loop(0, length, body, 0)

    others(owners, lambda owner: to_owner(owner).start())

    @pl.when(me < owners)
    def _():
        others(count, lambda source: from_source(source).wait_recv())
        mine[...] = in_ref[me]

        def add(source):
            mine[...] += held[source]

        others(count, add)
        others(count, lambda target: to_all(target).start())
        everyone[me] = mine[...]

    others(owners, lambda owner: to_owner(owner).wait_send())
    others(owners, lambda owner: from_owner(owner).wait_recv())

    @pl.when(me < owners)
    def _():
        others(count, lambda target: to_all(target).wait_send())

    raw = everyone[...].reshape(owners * 8, everyone.shape[2])
    factor = jnp.minimum(1.0, CLIP_NORM / jnp.sqrt(jnp.sum(raw * raw, keepdims=True) + 1e-6))
    scaled = raw * factor
    w_in_out[...] = scaled[0:features, :]
    b_in_out[...] = scaled[features : features + 1, :]
    w_out_out[...] = scaled[features + 1 : features + 10, :]


def shards(slabs, groups, eigvec, species, mode_cot, neighbours, pair_features, w_in, b_in, w_out):
    atoms, _, modes = eigvec.shape
    slot_count = neighbours.shape[1]
    rim = atoms // 2
    blocks, rim_blocks = atoms // TILE, rim // TILE
    features, hidden_width = w_in.shape

    inv_root = inverse_root_mass(species)
    panel = jnp.transpose(eigvec, (1, 0, 2))
    scaled = (panel.astype(jnp.float32) * inv_root[None, :, None]).astype(jnp.bfloat16)
    forward = [(i, (i + 1) % slabs) for i in range(slabs)]
    backward = [(target, source) for source, target in forward]
    low_rim = lax.ppermute(scaled[:, atoms - rim :, :], "slab", forward)
    high_rim = lax.ppermute(scaled[:, :rim, :], "slab", backward)
    nbr = neighbours.T
    cot = mode_cot[None, :]

    reach = 2 * rim_blocks
    own_tasks, low_tasks, high_tasks = [], [], []
    for block in range(blocks):
        for distance in range(reach + 1):
            partner = block + distance - rim_blocks
            if partner < 0:
                low_tasks.append((block, partner + rim_blocks, distance))
            elif partner < blocks:
                own_tasks.append((block, partner, distance))
            else:
                high_tasks.append((block, partner - blocks, distance))
    own_table, low_table, high_table = task_table(own_tasks), task_table(low_tasks), task_table(high_tasks)

    def band_scratch(parts):
        return [
            pltpu.VMEM((atoms, TILE), jnp.int32),
            pltpu.VMEM((atoms, TILE), jnp.int32),
            pltpu.VMEM((parts, atoms, TILE), jnp.float32),
            pltpu.VMEM((3 * TILE, 3 * TILE), jnp.float32),
            pltpu.VMEM((3 * TILE, 3 * TILE), jnp.float32),
        ]

    params = pltpu.CompilerParams(vmem_limit_bytes=VMEM_LIMIT)
    own_part = pl.pallas_call(
        own_kernel,
        out_shape=jax.ShapeDtypeStruct((atoms, 2 * TILE), jnp.float32),
        in_specs=[SMEM, VMEM, VMEM, VMEM],
        out_specs=VMEM,
        scratch_shapes=band_scratch(18),
        compiler_params=params,
        name="own_pairs",
    )(own_table, scaled, cot, nbr)
    pair_part = pl.pallas_call(
        rim_kernel,
        out_shape=jax.ShapeDtypeStruct((atoms, 2 * TILE), jnp.bfloat16),
        in_specs=[SMEM, SMEM] + [VMEM] * 6,
        out_specs=VMEM,
        scratch_shapes=band_scratch(9),
        compiler_params=params,
        name="rim_pairs",
    )(low_table, high_table, scaled, low_rim, high_rim, cot, nbr, own_part)

    share = atoms // groups
    pair_cot = pl.pallas_call(
        functools.partial(scatter_kernel, groups),
        out_shape=jax.ShapeDtypeStruct((share, 2 * TILE), jnp.float32),
        in_specs=[VMEM],
        out_specs=VMEM,
        scratch_shapes=[
            pltpu.VMEM((groups - 1, share, 2 * TILE), jnp.bfloat16),
            pltpu.SemaphoreType.DMA((groups - 1,)),
            pltpu.SemaphoreType.DMA((groups - 1,)),
        ],
        compiler_params=pltpu.CompilerParams(collective_id=0, has_side_effects=True),
        name="mode_scatter",
    )(pair_part.reshape(groups, share, 2 * TILE))

    w_rep = jnp.pad(jnp.repeat(w_out, slot_count, axis=0), ((0, 2 * TILE - 9 * slot_count), (0, 0)))
    owners = -(-(features + 10) // 8)
    features_grad, sums = pl.pallas_call(
        functools.partial(mlp_kernel, slot_count),
        out_shape=(
            jax.ShapeDtypeStruct(pair_features.shape, jnp.bfloat16),
            jax.ShapeDtypeStruct((owners * 8, hidden_width), jnp.float32),
        ),
        in_specs=[VMEM] * 5,
        out_specs=(VMEM, VMEM),
        scratch_shapes=[pltpu.VMEM((2 * TILE, hidden_width), jnp.float32)],
        compiler_params=params,
        name="pair_network",
    )(pair_features, pair_cot, w_in, b_in[None, :], w_rep)

    count = slabs * groups
    grad_w_in, grad_b_in, grad_w_out = pl.pallas_call(
        functools.partial(total_kernel, slabs, groups, features),
        out_shape=(
            jax.ShapeDtypeStruct((features, hidden_width), jnp.float32),
            jax.ShapeDtypeStruct((1, hidden_width), jnp.float32),
            jax.ShapeDtypeStruct((9, hidden_width), jnp.float32),
        ),
        in_specs=[VMEM],
        out_specs=(VMEM, VMEM, VMEM),
        scratch_shapes=[
            pltpu.VMEM((count, 8, hidden_width), jnp.float32),
            pltpu.VMEM((8, hidden_width), jnp.float32),
            pltpu.VMEM((owners, 8, hidden_width), jnp.float32),
            pltpu.SemaphoreType.DMA((owners,)),
            pltpu.SemaphoreType.DMA((count,)),
            pltpu.SemaphoreType.DMA((count,)),
            pltpu.SemaphoreType.DMA((owners,)),
        ],
        compiler_params=pltpu.CompilerParams(collective_id=1, has_side_effects=True),
        name="gradient_total",
    )(sums.reshape(owners, 8, hidden_width))
    return features_grad, grad_w_in, grad_b_in.reshape(hidden_width), grad_w_out


def solution(mesh):
    return jax.shard_map(
        functools.partial(shards, mesh.shape["slab"], mesh.shape["mode"]),
        mesh=mesh,
        in_specs=(
            P("slab", None, "mode"),
            P("slab"),
            P("mode"),
            P("slab", None),
            P(("slab", "mode"), None),
            P(),
            P(),
            P(),
        ),
        out_specs=(P(("slab", "mode"), None), P(), P(), P()),
        check_vma=False,
    )
```

time: 607 us -> 114 us (0.19)
  local copies, waits for them, and re-layouts: 301 us -> 7.04 us
  waiting for transfers between devices: 141 us -> 11.5 us
  Pallas kernels: 0 us -> 83.8 us
  matrix products: 73.4 us -> 0 us
  blocking collectives: 39.5 us -> 0 us
  other arithmetic: 25.4 us -> 2.73 us
  between operations: 16.1 us -> 0.7 us
    gather x20 -> x0, local copies, waits for them, and re-layouts: 187 us -> none  [fill_block(): jnp.take(extended, row_index.reshape(-1), axis=0)]
    pallas_call x0 -> x5, Pallas kernels: none -> 83.8 us  [the longest x1 29 us: shards(): pl.pallas_call(own_kernel, out_shape=jax.ShapeDtypeStruct((atoms, 2 * TIL...]
    psum x1 -> x0, waiting for transfers between devices: 80 us -> none  [shards(): lax.psum((part_w_in, part_b_in, part_w_out), ('slab', 'mode'))]
    dot_general x25 -> x0, matrix products: 73.4 us -> none  [the longest x10 36.9 us: fill_block(): lax.dot_general(left, partners, (((2,), (2,)), ((0,), (0,))), preferred_e...]
    dynamic_slice x30 -> x0, local copies, waits for them, and re-layouts: 43.4 us -> none  [the longest x20 25.4 us: fill_block(): own_rows = lax.dynamic_slice_in_dim(scaled, offset, block_size, 0)]
    psum x1 -> x0, blocking collectives: 39.5 us -> none  [shards(): lax.psum((part_w_in, part_b_in, part_w_out), ('slab', 'mode'))]
    ppermute x2, waiting for transfers between devices: 41.6 us -> 11.5 us  [the longest x1 9.32 us: shards(): low_rim = lax.ppermute(scaled[:, atoms - rim:, :], 'slab', forward)]
    transpose x20 -> x0, local copies, waits for them, and re-layouts: 19.3 us -> none  [the longest x10 10.3 us: fill_block(): self_terms = jnp.transpose(self_raw, (1, 2, 0)).reshape(9, block_size)]
  transfers between devices with their start and end apart: 4 -> 2, of which waited for: 4 -> 2; matrix products, arithmetic and copies ran while one was open for 1% -> 1% of each run, Pallas kernels for 0% -> 26%
where the time goes in v1:
time: 114 us; the launch traced here: 112 us
  Pallas kernels  83.8 us (74%)
  waiting for transfers between devices  11.5 us (10%)
  local copies, waits for them, and re-layouts  7.04 us (6%)
  starting transfers between devices  6.04 us (5%)
  other arithmetic  2.73 us (2%)
    pallas_call x1, Pallas kernels, shards(): pl.pallas_call(own_kernel, out_shape=jax.ShapeDtypeStruct((atoms, 2 * TIL...  29 us
    pallas_call x1, Pallas kernels, shards(): pl.pallas_call(functools.partial(total_kernel, slabs, groups, features),...  20 us
    pallas_call x1, Pallas kernels, shards(): pl.pallas_call(rim_kernel, out_shape=jax.ShapeDtypeStruct((atoms, 2 * TIL...  14.4 us
    pallas_call x1, Pallas kernels, shards(): pl.pallas_call(functools.partial(scatter_kernel, groups), out_shape=jax.S...  11 us
    pallas_call x1, Pallas kernels, shards(): pl.pallas_call(functools.partial(mlp_kernel, slot_count), out_shape=(jax....  9.46 us
    ppermute x1, waiting for transfers between devices, shards(): low_rim = lax.ppermute(scaled[:, atoms - rim:, :], 'slab', forward)  9.32 us
    unnamed x11, local copies, waits for them, and re-layouts  6.23 us
    ppermute x1, starting transfers between devices, shards(): high_rim = lax.ppermute(scaled[:, :rim, :], 'slab', backward)  3.04 us
  transfers between devices with their start and end apart: 2, of which 2 were waited for; matrix products, arithmetic and copies ran while one was open for 1% of the time, Pallas kernels for 26%

profile of v1, /device:TPU:0, one launch (start us, length us, event | category | flops | bytes accessed | tf_op | source)
XLA Modules:
  0.0 111.9 jit_solution(14005714267526409311)
XLA Ops:
  0.6 0.8 select_reduce_fusion
  1.4 1.9 %fusion.own_ref = bf16[3,1280,256]{2,1,0:T(8,128)(2,1)S(1)} fusion(bf16[1280,3,256]{2,0,1:T(8,128)(2,1)} %param.12, f32[1280]{0:T(1024)S(1)} %rsqrt.7), kind=kLoop, calls=%fused_computation.1 | loop fusion | flops 2949120 | bytes 3937280 | tf_op jit(solution)/shard_map/convert_element_type | solution.py:299
  3.4 0.0 copy-start
  3.4 0.0 copy-start.3
  3.4 0.1 fusion.1
  3.5 1.2 %copy-done = bf16[3,1280,256]{2,1,0:T(8,128)(2,1)} copy-done((bf16[3,1280,256]{2,1,0:T(8,128)(2,1)}, bf16[3,1280,256]{2,1,0:T(8,128)(2,1)S(1)}, u32[]{:S(2)}) %copy-start) | copy-done | bytes 1966104
  4.7 3.0 %collective-permute-start = (bf16[3,640,256]{2,1,0:T(8,128)(2,1)S(1)}, bf16[3,640,256]{2,1,0:T(8,128)(2,1)S(1)}, u32[]{:S(2)}, u32[]{:S(2)}) collective-permute-start(bf16[3,640,256]{2,1,0:T(8,128)(2,1)S(1)} %get-tuple-element.15), channel_id=1, source_target_pairs={{0,4},{4,8},{8,12},{12,16},{16,20},{20,24},{24,28},{28,0},{1,5},{5... | collective-permute-start | bytes 2949128 | tf_op jit(solution)/shard_map/ppermute | solution.py:302
  7.7 3.0 %collective-permute-start.1 = (bf16[3,640,256]{2,1,0:T(8,128)(2,1)S(1)}, bf16[3,640,256]{2,1,0:T(8,128)(2,1)S(1)}, u32[]{:S(2)}, u32[]{:S(2)}) collective-permute-start(bf16[3,640,256]{2,1,0:T(8,128)(2,1)S(1)} %get-tuple-element.14), channel_id=1, source_target_pairs={{4,0},{8,4},{12,8},{16,12},{20,16},{24,20},{28,24},{0,28},{5,1},{9... | collective-permute-start | bytes 2949128 | tf_op jit(solution)/shard_map/ppermute | solution.py:303
  10.7 0.0 copy-done.3
  10.8 0.7 pad.4.w_rep_ref
  11.4 29.0 %own_pairs.1.part_ref = f32[1280,256]{1,0:T(8,128)} custom-call(s32[3,81]{1,0:T(4,128)} %constant.15.clone.table, bf16[3,1280,256]{2,1,0:T(8,128)(2,1)} %copy-done, f32[1,256]{1,0:T(1,128)} %bitcast.14, s32[16,1280]{1,0:T(8,128)} %bitcast.10), custom_call_target="tpu_custom_call" | custom-call | tf_op jit(solution)/shard_map/own_pairs/pallas_call | solution.py:330
  40.5 9.3 %collective-permute-done.low_rim = bf16[3,640,256]{2,1,0:T(8,128)(2,1)S(1)} collective-permute-done((bf16[3,640,256]{2,1,0:T(8,128)(2,1)S(1)}, bf16[3,640,256]{2,1,0:T(8,128)(2,1)S(1)}, u32[]{:S(2)}, u32[]{:S(2)}) %collective-permute-start) | collective-permute-done | bytes 983072 | tf_op jit(solution)/shard_map/ppermute | solution.py:302
  49.8 0.0 copy-start.1
  49.8 2.2 %collective-permute-done.1.high_rim = bf16[3,640,256]{2,1,0:T(8,128)(2,1)S(1)} collective-permute-done((bf16[3,640,256]{2,1,0:T(8,128)(2,1)S(1)}, bf16[3,640,256]{2,1,0:T(8,128)(2,1)S(1)}, u32[]{:S(2)}, u32[]{:S(2)}) %collective-permute-start.1) | collective-permute-done | bytes 983072 | tf_op jit(solution)/shard_map/ppermute | solution.py:303
  52.0 0.0 copy-done.1
  52.0 0.0 copy-start.2
  52.0 0.9 copy-done.2
  52.9 14.4 %rim_pairs.1 = bf16[1280,256]{1,0:T(8,128)(2,1)} custom-call(s32[3,17]{1,0:T(4,128)} %constant.16.clone.low_table, s32[3,17]{1,0:T(4,128)} %constant.17.clone.high_table, bf16[3,1280,256]{2,1,0:T(8,128)(2,1)} %copy-done, bf16[3,640,256]{2,1,0:T(8,128)(2,1)} %copy-done.1, bf16[3,640,256]{2,1,0:T(8,128)(2,1)} %copy-done.2, f32[1,256]{1,0:T(1,128)} %bitcast.15, ...), custom_call_target="tpu_custom_call" | custom-call | tf_op jit(solution)/shard_map/rim_pairs/pallas_call | solution.py:339
  67.3 11.0 %mode_scatter.1.cot_ref = f32[320,256]{1,0:T(8,128)} custom-call(bf16[4,320,256]{2,1,0:T(8,128)(2,1)} %bitcast.9), custom_call_target="tpu_custom_call" | custom-call | tf_op jit(solution)/shard_map/mode_scatter/pallas_call | solution.py:350
  78.3 9.5 %pair_network.1 = (bf16[5120,128]{1,0:T(8,128)(2,1)}, f32[144,256]{1,0:T(8,128)}) custom-call(bf16[5120,128]{1,0:T(8,128)(2,1)} %x_ref.1, f32[320,256]{1,0:T(8,128)} %mode_scatter.1.cot_ref, bf16[128,256]{1,0:T(8,128)(2,1)} %w_in_ref.1, f32[1,256]{1,0:T(1,128)} %bitcast.16, bf16[256,256]{1,0:T(8,128)(2,1)} %pad.4.w_rep_ref), custom_call_target="tpu_custom_call" | custom-call | tf_op jit(solution)/shard_map/pair_network/pallas_call | solution.py:366
  87.8 20.0 %gradient_total.1 = (f32[128,256]{1,0:T(8,128)}, f32[1,256]{1,0:T(1,128)}, f32[9,256]{1,0:T(8,128)}) custom-call(f32[18,8,256]{2,1,0:T(8,128)} %bitcast.13), custom_call_target="tpu_custom_call" | custom-call | tf_op jit(solution)/shard_map/gradient_total/pallas_call | solution.py:380
  107.7 1.6 %copy.19 = f32[128,256]{1,0:T(8,128)} copy(f32[128,256]{1,0:T(8,128)} %get-tuple-element.21) | data formatting | bytes 262144
  109.3 1.2 %copy.20 = f32[256]{0:T(256)} copy(f32[256]{0:T(256)} %bitcast.17) | data formatting | bytes 2048
  110.5 1.3 %copy.21 = f32[9,256]{1,0:T(8,128)} copy(f32[9,256]{1,0:T(8,128)} %get-tuple-element.23) | data formatting | bytes 18432
  (2 shorter events, 0.0 us)
Async XLA Ops:
  3.4 1.3 %copy-start = (bf16[3,1280,256]{2,1,0:T(8,128)(2,1)}, bf16[3,1280,256]{2,1,0:T(8,128)(2,1)S(1)}, u32[]{:S(2)}) copy-start(bf16[3,1280,256]{2,1,0:T(8,128)(2,1)S(1)} %fusion.own_ref) | copy-start | bytes 5898244
  3.4 7.3 %copy-start.3 = (bf16[9,256]{1,0:T(8,128)(2,1)S(1)}, bf16[9,256]{1,0:T(8,128)(2,1)}, u32[]{:S(2)}) copy-start(bf16[9,256]{1,0:T(8,128)(2,1)} %param.19) | copy-start | bytes 13828
  4.7 45.1 %collective-permute-start = (bf16[3,640,256]{2,1,0:T(8,128)(2,1)S(1)}, bf16[3,640,256]{2,1,0:T(8,128)(2,1)S(1)}, u32[]{:S(2)}, u32[]{:S(2)}) collective-permute-start(bf16[3,640,256]{2,1,0:T(8,128)(2,1)S(1)} %get-tuple-element.15), channel_id=1, source_target_pairs={{0,4},{4,8},{8,12},{12,16},{16,20},{20,24},{24,28},{28,0},{1,5},{5... | collective-permute-start | bytes 2949128 | tf_op jit(solution)/shard_map/ppermute | solution.py:302
  7.7 44.3 %collective-permute-start.1 = (bf16[3,640,256]{2,1,0:T(8,128)(2,1)S(1)}, bf16[3,640,256]{2,1,0:T(8,128)(2,1)S(1)}, u32[]{:S(2)}, u32[]{:S(2)}) collective-permute-start(bf16[3,640,256]{2,1,0:T(8,128)(2,1)S(1)} %get-tuple-element.14), channel_id=1, source_target_pairs={{4,0},{8,4},{12,8},{16,12},{20,16},{24,20},{28,24},{0,28},{5,1},{9... | collective-permute-start | bytes 2949128 | tf_op jit(solution)/shard_map/ppermute | solution.py:303
  49.8 2.2 %copy-start.1 = (bf16[3,640,256]{2,1,0:T(8,128)(2,1)}, bf16[3,640,256]{2,1,0:T(8,128)(2,1)S(1)}, u32[]{:S(2)}) copy-start(bf16[3,640,256]{2,1,0:T(8,128)(2,1)S(1)} %collective-permute-done.low_rim) | copy-start | bytes 2949124
  52.0 0.9 copy-start.2
